TPU v7x, 32 devices: a whole 2x2x4 slice. The times are simulated.
32 devices in a mesh: tm: 4 (over z), rows: 8 (over y, x, core).
Axes of the slice: x: 2, y: 2, z: 4, core: 2. Of those that a mesh axis runs over, the one named last changes fastest.
Arguments:
- snapshots: float32 [196608, 256], P('rows', 'tm'), may hold values from -100 to 100
- last_snapshot: float32 [196608], P('rows'), may hold values from -100 to 100
Outputs:
- basis_rows: float32 [8, 4, 6144, 256], P('rows', 'tm')
- factor: float32 [256, 256], replicated
- projected: float32 [256, 256], replicated
- operator: float32 [256, 256], replicated
All inputs are finite; a program needn't handle non-finite values.
Results may differ from a plain program's by a relative error of at most 0.0003.
Values sent between devices are 32-bit elements; how exact they have to be, the bound alone decides.
No kernel may reach another device: no remote copies, remote signals or barrier semaphores. Data moves between devices by JAX's collectives and lax.ppermute only.
A program may use at most 128 MiB of HBM per device.

v0:
```python
import jax
import jax.numpy as jnp
from jax import lax
from jax.sharding import PartitionSpec as P


def sum_moments(first_part, second_part):
    first_total, second_total = lax.psum((first_part, second_part), ("tm", "rows"))
    return (first_total, second_total)


def shards(snapshots, last_snapshot):
    highest = lax.Precision.HIGHEST
    local_rows = lax.all_to_all(snapshots, "tm", split_axis=0, concat_axis=1, tiled=True)
    row_count = local_rows.shape[0]
    col_count = local_rows.shape[1]
    last_column = lax.dynamic_slice_in_dim(
        last_snapshot, lax.axis_index("tm") * row_count, row_count, 0
    )
    gram_part = jnp.dot(
        local_rows.T, local_rows, precision=highest, preferred_element_type=jnp.float32
    )
    tail_part = jnp.dot(
        last_column, local_rows, precision=highest, preferred_element_type=jnp.float32
    )
    gram_total, tail_total = sum_moments(gram_part, tail_part)
    samples = row_count * lax.axis_size("tm") * lax.axis_size("rows")
    gram_matrix = gram_total / samples
    tail_column = tail_total / samples
    cross_matrix = jnp.concatenate([gram_matrix[:, 1:], tail_column[:, None]], axis=1)
    lower_factor = jnp.linalg.cholesky(gram_matrix)
    identity = jnp.eye(col_count, dtype=jnp.float32)
    inverse = jax.scipy.linalg.solve_triangular(lower_factor, identity, lower=True)
    factor = lower_factor.T
    basis_rows = jnp.dot(
        local_rows, inverse.T, precision=highest, preferred_element_type=jnp.float32
    )
    projected = jnp.dot(
        inverse, cross_matrix, precision=highest, preferred_element_type=jnp.float32
    )
    operator = jnp.dot(projected, inverse.T, precision=highest, preferred_element_type=jnp.float32)
    return (basis_rows.reshape(1, 1, row_count, col_count), factor, projected, operator)


def solution(mesh):
    in_specs = (P("rows", "tm"), P("rows"))
    out_specs = (P("rows", "tm", None, None), P(), P(), P())
    return jax.shard_map(shards, mesh=mesh, in_specs=in_specs, out_specs=out_specs, check_vma=False)
```

profile of v0, /device:TPU:0, one launch (start us, length us, event | category | flops | bytes accessed | tf_op | source)
XLA Modules:
  0.0 436.9 jit_solution(7543601814728142755)
XLA Ops:
  7.2 0.0 copy-start
  7.2 6.2 %copy.27 = f32[8,4,8,6144]{3,2,0,1:T(8,128)} copy(f32[8,4,8,6144]{3,2,1,0:T(8,128)} %bitcast.54) | data formatting | bytes 12582912 | tf_op jit(solution)/shard_map/all_to_all | solution.py:14
  13.4 6.3 %all-to-all-start = ((f32[4,6144,64]{1,2,0:T(8,128)}), f32[4,6144,64]{1,2,0:T(8,128)}, u32[]{:S(2)}, u32[]{:S(2)}) async-start(f32[4,6144,64]{1,2,0:T(8,128)} %bitcast.53), calls=%async_computation | async-start | bytes 12582912 | tf_op jit(solution)/shard_map/all_to_all | solution.py:14
  19.7 0.0 all-reduce.3.cloned.1.call-start
  19.7 0.0 copy-done
  19.8 138.7 %all-to-all-done = f32[4,6144,64]{1,2,0:T(8,128)} async-done(((f32[4,6144,64]{1,2,0:T(8,128)}), f32[4,6144,64]{1,2,0:T(8,128)}, u32[]{:S(2)}, u32[]{:S(2)}) %all-to-all-start) | async-done | bytes 6291488 | tf_op jit(solution)/shard_map/all_to_all | solution.py:14
  158.4 17.7 %fusion.19 = f32[256,256]{0,1:T(8,128)} fusion(f32[6144,256]{0,1:T(8,128)} %bitcast.1), kind=kOutput, calls=%fused_computation.44 | convolution fusion | flops 4831838208 | bytes 6553600 | tf_op jit(solution)/shard_map/dot_general | solution.py:20
  176.2 7.0 %fusion.20 = f32[1,256]{1,0:T(1,128)S(1)} fusion(f32[6144,1]{0,1:T(1,128)S(1)} %bitcast.55, f32[6144,256]{0,1:T(8,128)} %bitcast.1), kind=kOutput, calls=%fused_computation.45 | convolution fusion | flops 18874368 | bytes 6317056 | tf_op jit(solution)/shard_map/dot_general | solution.py:23
  183.1 38.1 %psum.15 = f32[256]{0:T(256)S(1)} all-reduce(f32[256]{0:T(256)S(1)} %bitcast.57), channel_id=1, replica_groups=mesh['tm'=4,'rows'=8] {'tm','rows'}, use_global_device_ids=true, to_apply=%region_5.6 | all-reduce | flops 256 | bytes 2048 | tf_op jit(solution)/shard_map/psum | solution.py:8
  221.2 0.0 all-reduce.3.cloned.1.call-update
  221.2 125.6 %all-reduce.3.cloned.1.call-done = f32[256,256]{0,1:T(8,128)} async-done(((f32[256,256]{0,1:T(8,128)}), f32[256,256]{0,1:T(8,128)}) %all-reduce.3.cloned.1.call-update) | async-done | bytes 262160 | tf_op jit(solution)/shard_map/psum | solution.py:8
  346.8 1.0 broadcast_multiply_fusion
  347.8 0.1 copy.21
  347.9 1.0 fusion.4
  348.9 11.7 %cholesky.50 = f32[128,128]{1,0:T(8,128)S(1)} custom-call(f32[128,128]{1,0:T(8,128)S(1)} %cholesky.118), custom_call_target="Cholesky" | custom-call | tf_op jit(solution)/shard_map/jit(cholesky)/cholesky | solution.py:31
  360.7 9.8 %custom-call.15 = f32[1,128,128]{1,2,0:T(8,128)S(1)} custom-call(f32[1,128,128]{2,1,0:T(8,128)S(1)} %get-tuple-element.43), custom_call_target="InvertDiagBlocksLowerTriangular" | custom-call | tf_op jit(solution)/shard_map/jit(cholesky)/cholesky | solution.py:31
  370.5 0.2 constant_dynamic-update-slice_fusion.1
  370.8 0.3 convolution_subtract_fusion.1
  371.0 11.7 %cholesky.105 = f32[128,128]{1,0:T(8,128)S(1)} custom-call(f32[128,128]{1,0:T(8,128)S(1)} %convolution_subtract_fusion.1), custom_call_target="Cholesky" | custom-call | tf_op jit(solution)/shard_map/jit(cholesky)/cholesky | solution.py:31
  382.8 0.6 compare_reduce_fusion
  384.8 0.8 copy.23
  385.6 0.1 triangular_solve.63
  385.7 4.0 while.1
  385.7 0.6 fusion.32
  386.3 1.4 bitcast_dynamic-update-slice_fusion.2
  387.7 0.6 fusion.32
  388.3 1.4 bitcast_dynamic-update-slice_fusion.2
  389.7 19.9 %custom-call.16 = f32[2,128,128]{1,2,0:T(8,128)S(1)} custom-call(f32[2,128,128]{2,1,0:T(8,128)S(1)} %get-tuple-element.11), custom_call_target="InvertDiagBlocksLowerTriangular" | custom-call | tf_op jit(solution)/shard_map/jit(_solve_triangular)/triangular_solve | solution.py:33
  409.6 0.3 fusion.8
  409.8 0.3 convolution_subtract_fusion
  410.1 0.3 fusion.11
  410.4 11.5 %convolution_bitcast_fusion = f32[1,1,6144,256]{2,3,1,0:T(8,128)} fusion(f32[6144,256]{0,1:T(8,128)} %bitcast.1, f32[128,256]{1,0:T(8,128)S(1)} %fusion.11, f32[128,256]{1,0:T(8,128)S(1)} %fusion.8), kind=kOutput, calls=%fused_computation.2 | convolution fusion | flops 4831903744 | bytes 12845056 | tf_op jit(solution)/shard_map/dot_general | solution.py:35
  421.9 0.4 fusion
  422.3 0.0 copy-start.1
  422.4 1.1 fusion.7
  423.5 6.6 %copy.22 = f32[1,1,6144,256]{3,2,1,0:T(8,128)} copy(f32[1,1,6144,256]{2,3,1,0:T(8,128)} %convolution_bitcast_fusion) | data formatting | bytes 12582912
  430.0 0.0 copy-done.1
  (13 shorter events, 0.2 us)
Async XLA Ops:
  7.2 12.5 %copy-start = (f32[24576]{0:T(1024)S(1)}, f32[24576]{0:T(1024)}, u32[]{:S(2)}) copy-start(f32[24576]{0:T(1024)} %param.3) | copy-start | bytes 294916
  13.4 145.1 %all-to-all-start = ((f32[4,6144,64]{1,2,0:T(8,128)}), f32[4,6144,64]{1,2,0:T(8,128)}, u32[]{:S(2)}, u32[]{:S(2)}) async-start(f32[4,6144,64]{1,2,0:T(8,128)} %bitcast.53), calls=%async_computation | async-start | bytes 12582912 | tf_op jit(solution)/shard_map/all_to_all | solution.py:14
  19.7 327.1 %all-reduce.3.cloned.1.call-start = ((), (), s32[]{:S(2)}) async-start(), calls=%async_computation.1 | async-start | bytes 524288 | tf_op jit(solution)/shard_map/psum | solution.py:8
  422.3 7.7 %copy-start.1 = (f32[256,256]{1,0:T(8,128)}, f32[256,256]{1,0:T(8,128)S(1)}, u32[]{:S(2)}) copy-start(f32[256,256]{1,0:T(8,128)S(1)} %fusion) | copy-start | bytes 786436
Sparse Core Ops, SparseCore 0:
  221.4 125.3 all-reduce.2
where the time goes:
time: 437 us
  waiting for transfers between devices  264 us (60%)
  other arithmetic  55.9 us (13%)
  matrix products  39 us (9%)
  blocking collectives  38.1 us (9%)
  local copies, waits for them, and re-layouts  17.8 us (4%)
  between operations  15.5 us (4%)
  starting transfers between devices  6.32 us (1%)
    all_to_all x1, waiting for transfers between devices, shards(): lax.all_to_all(snapshots, 'tm', split_axis=0, concat_axis=1, tiled=True)  139 us
    psum x1, waiting for transfers between devices, sum_moments(): lax.psum((first_part, second_part), ('tm', 'rows'))  126 us
    psum x1, blocking collectives, sum_moments(): lax.psum((first_part, second_part), ('tm', 'rows'))  38.1 us
    another operation x6, other arithmetic, shards(): lower_factor = jnp.linalg.cholesky(gram_matrix)  34 us
    another operation x2, other arithmetic, shards(): jax.scipy.linalg.solve_triangular(lower_factor, identity, lower=True)  19.9 us
    dot_general x1, matrix products, shards(): jnp.dot(local_rows.T, local_rows, precision=highest, preferred_element_ty...  17.7 us
    dot_general x1, matrix products, shards(): jnp.dot(local_rows, inverse.T, precision=highest, preferred_element_type=...  11.5 us
  transfers between devices with their start and end apart: 2, of which 2 were waited for; matrix products, arithmetic and copies ran while one was open for 0% of the time, Pallas kernels for 0%

commit v1 on v0

--- a/solution.py
+++ b/solution.py
@@ -5,7 +5,7 @@
 
 
 def sum_moments(first_part, second_part):
-    first_total, second_total = lax.psum((first_part, second_part), ("tm", "rows"))
+    first_total, second_total = lax.psum(lax.psum((first_part, second_part), "rows"), "tm")
     return (first_total, second_total)
 
 

time: 437 us -> 344 us (0.79)
  waiting for transfers between devices: 264 us -> 59.1 us
  blocking collectives: 38.1 us -> 168 us
  matrix products: 39 us -> 27.3 us
  starting transfers between devices: 6.32 us -> 0.08 us
    all_to_all x0 -> x1, blocking collectives: none -> 144 us  [shards(): lax.all_to_all(snapshots, 'tm', split_axis=0, concat_axis=1, tiled=True)]
    all_to_all x1 -> x0, waiting for transfers between devices: 139 us -> none  [shards(): lax.all_to_all(snapshots, 'tm', split_axis=0, concat_axis=1, tiled=True)]
    psum x1 -> x2, waiting for transfers between devices: 126 us -> 59.1 us  [the longest x1 53 us: sum_moments(): lax.psum((first_part, second_part), 'rows')]
    psum x1 -> x2, blocking collectives: 38.1 us -> 24.1 us  [the longest x1 12.3 us: sum_moments(): lax.psum(lax.psum((first_part, second_part), 'rows'), 'tm')]
    dot_general x1, matrix products: 17.7 us -> 5.89 us  [shards(): jnp.dot(local_rows.T, local_rows, precision=highest, preferred_element_ty...]
    all_to_all x1 -> x0, starting transfers between devices: 6.32 us -> none  [shards(): lax.all_to_all(snapshots, 'tm', split_axis=0, concat_axis=1, tiled=True)]
    unnamed x6 -> x8, local copies, waits for them, and re-layouts: 7.41 us -> 10.1 us
  transfers between devices with their start and end apart: 2 -> 2, of which waited for: 2 -> 2; matrix products, arithmetic and copies ran while one was open for 0% -> 2% of each run, Pallas kernels for 0% -> 0%
where the time goes in v1:
time: 344 us
  blocking collectives  168 us (49%)
  waiting for transfers between devices  59.1 us (17%)
  other arithmetic  55.9 us (16%)
  matrix products  27.3 us (8%)
  local copies, waits for them, and re-layouts  17.6 us (5%)
  between operations  15.5 us (5%)
    all_to_all x1, blocking collectives, shards(): lax.all_to_all(snapshots, 'tm', split_axis=0, concat_axis=1, tiled=True)  144 us
    psum x1, waiting for transfers between devices, sum_moments(): lax.psum((first_part, second_part), 'rows')  53 us
    another operation x6, other arithmetic, shards(): lower_factor = jnp.linalg.cholesky(gram_matrix)  34 us
    another operation x2, other arithmetic, shards(): jax.scipy.linalg.solve_triangular(lower_factor, identity, lower=True)  19.9 us
    psum x1, blocking collectives, sum_moments(): lax.psum(lax.psum((first_part, second_part), 'rows'), 'tm')  12.3 us
    psum x1, blocking collectives, sum_moments(): lax.psum((first_part, second_part), 'rows')  11.8 us
    dot_general x1, matrix products, shards(): jnp.dot(local_rows, inverse.T, precision=highest, preferred_element_type=...  11.6 us
    unnamed x8, local copies, waits for them, and re-layouts  10.1 us
  transfers between devices with their start and end apart: 2, of which 2 were waited for; matrix products, arithmetic and copies ran while one was open for 2% of the time, Pallas kernels for 0%

profile of v1, /device:TPU:0, one launch (start us, length us, event | category | flops | bytes accessed | tf_op | source)
XLA Modules:
  0.0 343.9 jit_solution(687304196923190433)
XLA Ops:
  7.2 0.0 copy-start
  7.2 0.0 all-reduce.4.cloned.1.call-start
  7.2 3.2 copy.27
  10.5 144.2 %all_to_all.19 = f32[4,6144,64]{1,2,0:T(8,128)S(1)} all-to-all(f32[4,6144,64]{1,2,0:T(8,128)S(1)} %bitcast.56), channel_id=1, replica_groups=mesh['tm'=4,'rows'=8] {'tm'}, dimensions={0} | all-to-all | bytes 12582912 | tf_op jit(solution)/shard_map/all_to_all | solution.py:14
  154.7 0.0 copy-start.1
  154.7 2.7 copy-done.1
  157.4 5.9 %fusion.19 = f32[256,256]{0,1:T(8,128)} fusion(f32[6144,256]{0,1:T(8,128)S(1)} %bitcast.53), kind=kOutput, calls=%fused_computation.44 | convolution fusion | flops 4831838208 | bytes 6553600 | tf_op jit(solution)/shard_map/dot_general | solution.py:20
  163.3 0.0 all-reduce.4.cloned.1.call-update
  163.3 0.0 all-reduce.6.cloned.1.call-start
  163.4 0.0 copy-done
  163.4 53.0 %all-reduce.4.cloned.1.call-done = f32[256,256]{0,1:T(8,128)} async-done(((f32[256,256]{0,1:T(8,128)}), f32[256,256]{0,1:T(8,128)}) %all-reduce.4.cloned.1.call-update) | async-done | bytes 262160 | tf_op jit(solution)/shard_map/psum | solution.py:8
  216.5 0.0 all-reduce.6.cloned.1.call-update
  216.5 7.0 %fusion.20 = f32[1,256]{1,0:T(1,128)S(1)} fusion(f32[6144,1]{0,1:T(1,128)S(1)} %bitcast.58, f32[6144,256]{0,1:T(8,128)} %bitcast.54), kind=kOutput, calls=%fused_computation.45 | convolution fusion | flops 18874368 | bytes 6317056 | tf_op jit(solution)/shard_map/dot_general | solution.py:23
  223.5 11.8 %psum.30 = f32[256]{0:T(256)S(1)} all-reduce(f32[256]{0:T(256)S(1)} %bitcast.60), channel_id=1, replica_groups=mesh['tm'=4,'rows'=8] {'rows'}, use_global_device_ids=true, to_apply=%region_6.7 | all-reduce | flops 256 | bytes 2048 | tf_op jit(solution)/shard_map/psum | solution.py:8
  235.3 12.3 %psum.31 = f32[256]{0:T(256)S(1)} all-reduce(f32[256]{0:T(256)S(1)} %psum.30), channel_id=1, replica_groups=mesh['tm'=4,'rows'=8] {'tm'}, use_global_device_ids=true, to_apply=%region_7.8 | all-reduce | flops 256 | bytes 2048 | tf_op jit(solution)/shard_map/psum | solution.py:8
  247.5 6.1 %all-reduce.6.cloned.1.call-done = f32[256,256]{0,1:T(8,128)} async-done(((f32[256,256]{0,1:T(8,128)}), f32[256,256]{0,1:T(8,128)}) %all-reduce.6.cloned.1.call-update) | async-done | bytes 262160 | tf_op jit(solution)/shard_map/psum | solution.py:8
  253.6 1.0 broadcast_multiply_fusion
  254.6 0.1 copy.21
  254.7 1.0 fusion.4
  255.8 11.7 %cholesky.50 = f32[128,128]{1,0:T(8,128)S(1)} custom-call(f32[128,128]{1,0:T(8,128)S(1)} %cholesky.118), custom_call_target="Cholesky" | custom-call | tf_op jit(solution)/shard_map/jit(cholesky)/cholesky | solution.py:31
  267.5 9.8 %custom-call.15 = f32[1,128,128]{1,2,0:T(8,128)S(1)} custom-call(f32[1,128,128]{2,1,0:T(8,128)S(1)} %get-tuple-element.43), custom_call_target="InvertDiagBlocksLowerTriangular" | custom-call | tf_op jit(solution)/shard_map/jit(cholesky)/cholesky | solution.py:31
  277.3 0.2 constant_dynamic-update-slice_fusion.1
  277.6 0.3 convolution_subtract_fusion.1
  277.8 11.7 %cholesky.105 = f32[128,128]{1,0:T(8,128)S(1)} custom-call(f32[128,128]{1,0:T(8,128)S(1)} %convolution_subtract_fusion.1), custom_call_target="Cholesky" | custom-call | tf_op jit(solution)/shard_map/jit(cholesky)/cholesky | solution.py:31
  289.6 0.6 compare_reduce_fusion
  291.6 0.8 copy.23
  292.4 0.1 triangular_solve.63
  292.5 4.1 %while.1 = (s32[]{:T(128)}, f32[256,256]{1,0:T(8,128)S(1)}, s32[2,2]{1,0:T(2,128)S(1)}, f32[2,128,128]{2,1,0:T(8,128)S(1)}, s32[]{:T(128)}) while((s32[]{:T(128)}, f32[256,256]{1,0:T(8,128)S(1)}, s32[2,2]{1,0:T(2,128)S(1)}, f32[2,128,128]{2,1,0:T(8,128)S(1)}, s32[]{:T(128)}) %tuple.32), condition=%wide.while_cond, body=%wide.while_body.sunk | while | flops 2 | bytes 131189 | solution.py:33
  292.5 0.6 fusion.32
  293.1 1.4 bitcast_dynamic-update-slice_fusion.2
  294.5 0.6 fusion.32
  295.1 1.4 bitcast_dynamic-update-slice_fusion.2
  296.6 19.9 %custom-call.16 = f32[2,128,128]{1,2,0:T(8,128)S(1)} custom-call(f32[2,128,128]{2,1,0:T(8,128)S(1)} %get-tuple-element.11), custom_call_target="InvertDiagBlocksLowerTriangular" | custom-call | tf_op jit(solution)/shard_map/jit(_solve_triangular)/triangular_solve | solution.py:33
  316.5 0.3 fusion.8
  316.8 0.3 convolution_subtract_fusion
  317.0 0.3 fusion.11
  317.3 11.6 %convolution_bitcast_fusion = f32[1,1,6144,256]{2,3,1,0:T(8,128)} fusion(f32[6144,256]{0,1:T(8,128)} %bitcast.55, f32[128,256]{1,0:T(8,128)S(1)} %fusion.11, f32[128,256]{1,0:T(8,128)S(1)} %fusion.8), kind=kOutput, calls=%fused_computation.2 | convolution fusion | flops 4831903744 | bytes 12845056 | tf_op jit(solution)/shard_map/dot_general | solution.py:35
  328.9 0.4 fusion
  329.3 0.0 copy-start.2
  329.4 1.1 fusion.7
  330.5 6.6 %copy.22 = f32[1,1,6144,256]{3,2,1,0:T(8,128)} copy(f32[1,1,6144,256]{2,3,1,0:T(8,128)} %convolution_bitcast_fusion) | data formatting | bytes 12582912
  337.0 0.0 copy-done.2
  (13 shorter events, 0.2 us)
Async XLA Ops:
  7.2 156.2 %copy-start = (f32[24576]{0:T(1024)S(1)}, f32[24576]{0:T(1024)}, u32[]{:S(2)}) copy-start(f32[24576]{0:T(1024)} %param.3) | copy-start | bytes 294916
  7.2 209.3 %all-reduce.4.cloned.1.call-start = ((), (), s32[]{:S(2)}) async-start(), calls=%async_computation.1 | async-start | bytes 524288 | tf_op jit(solution)/shard_map/psum | solution.py:8
  154.7 2.7 copy-start.1
  163.3 90.3 %all-reduce.6.cloned.1.call-start = ((), (), s32[]{:S(2)}) async-start(), calls=%async_computation.2 | async-start | bytes 524288 | tf_op jit(solution)/shard_map/psum | solution.py:8
  329.3 7.7 %copy-start.2 = (f32[256,256]{1,0:T(8,128)}, f32[256,256]{1,0:T(8,128)S(1)}, u32[]{:S(2)}) copy-start(f32[256,256]{1,0:T(8,128)S(1)} %fusion) | copy-start | bytes 786436
Sparse Core Ops, SparseCore 0:
  163.4 53.0 all-reduce.3
  218.9 34.6 all-reduce.5
